TPU v7x, 32 devices: a whole 2x2x4 slice. The times are simulated.
32 devices in a mesh: batch: 4 (over z), seq: 8 (over y, x, core).
Axes of the slice: x: 2, y: 2, z: 4, core: 2. Of those that a mesh axis runs over, the one named last changes fastest.
Arguments:
- inputs: float32 [8, 1024, 768], P('batch', 'seq'), may hold values from -6 to 6
- cotangent: float32 [8, 1024, 768], P('batch', 'seq'), may hold values from -6 to 6
- lengths: int32 [8], P('batch'), may hold values from 256 to 1024, as said below
- joint_weight: bfloat16 [768, 2304], P(('batch', 'seq')), may hold values from -0.3125 to 0.3125
- output_weight: bfloat16 [768, 768], P(('batch', 'seq')), may hold values from -1.25 to 1.25
- vectors: bfloat16 [8, 768], P(None, ('batch', 'seq')), may hold values from -2 to 2
- expand_weight: bfloat16 [768, 3072], P(('batch', 'seq')), may hold values from -0.21875 to 0.21875
- expand_bias: bfloat16 [3072], P(('batch', 'seq')), may hold values from -1.1953125 to 1.1953125
- reduce_weight: bfloat16 [3072, 768], P(('batch', 'seq')), may hold values from -0.15625 to 0.15625
Outputs:
- result: float32 [8, 1024, 768], P('batch', 'seq')
- grad_inputs: float32 [8, 1024, 768], P('batch', 'seq')
- grad_joint: float32 [768, 2304], P(('batch', 'seq'))
- grad_output: float32 [768, 768], P(('batch', 'seq'))
- grad_vectors: float32 [8, 768], P(None, ('batch', 'seq'))
- grad_expand: float32 [768, 3072], P(('batch', 'seq'))
- grad_expand_bias: float32 [3072], P(('batch', 'seq'))
- grad_reduce: float32 [3072, 768], P(('batch', 'seq'))
Inputs may be any that keep to these rules, and one draw needn't show every extreme that they name: `lengths`: some sequence is full (1024 valid tokens) in every draw.
All inputs are finite; a program needn't handle non-finite values.
Results may differ from a plain program's by a relative error of at most 0.018.
The roundings to bfloat16 on the way count: a program that leaves them out, or rounds other values in their place, can miss the bound.
Values may be sent and summed in bfloat16 or wider, within the bound.
A program may use at most 192 MiB of HBM per device.

v0:
```python
import math
import jax
import jax.numpy as jnp
from jax import lax
from jax.sharding import PartitionSpec as P

HEADS = 12
HEAD_DIM = 64
EPSILON = 1e-12
SCORE_SCALE = 0.125
NEG_FILL = -1e30
HALF_ROOT = 0.7071067811865476
INV_ROOT_TAU = 0.3989422804014327
block_limit = 256


def layer_norm(residual, norm_gain, norm_shift):
    centered = residual - jnp.mean(residual, axis=-1, keepdims=True)
    inverse = lax.rsqrt(jnp.mean(centered * centered, axis=-1, keepdims=True) + EPSILON)
    normed = centered * inverse
    return (normed * norm_gain + norm_shift, normed, inverse)


def norm_back(grad_out, normed, inverse, norm_gain):
    grad_normed = grad_out * norm_gain
    mean_grad = jnp.mean(grad_normed, axis=-1, keepdims=True)
    mean_proj = jnp.mean(grad_normed * normed, axis=-1, keepdims=True)
    grad_in = inverse * (grad_normed - mean_grad - normed * mean_proj)
    return (grad_in, jnp.sum(grad_out * normed, axis=0), jnp.sum(grad_out, axis=0))


def gelu_value(before_gelu):
    return 0.5 * before_gelu * (1.0 + lax.erf(before_gelu * HALF_ROOT))


def gelu_slope(before_gelu):
    return (
        0.5 * (1.0 + lax.erf(before_gelu * HALF_ROOT))
        + before_gelu * jnp.exp(-0.5 * before_gelu * before_gelu) * INV_ROOT_TAU
    )


def over_blocks(piece_rows, block_fn, carried):
    block_size = math.gcd(piece_rows, block_limit)

    def run_block(block_index, current):
        return block_fn(current, block_index * block_size, block_size)

    return lax.fori_loop(0, piece_rows // block_size, run_block, carried)


def head_scores(left_heads, right_heads, right_places, lengths):
    scores = (
        jnp.einsum("sqhd,skhd->shqk", left_heads, right_heads, preferred_element_type=jnp.float32)
        * SCORE_SCALE
    )
    allowed = right_places[None, :] < lengths[:, None]
    return jnp.where(allowed[:, None, None, :], scores, NEG_FILL)


def cut_heads(gathered_piece, offset, block_size, head_count):
    sliced = lax.dynamic_slice_in_dim(gathered_piece, offset, block_size, 1)
    return sliced.reshape(sliced.shape[0], block_size, head_count, -1)


def gather_attention(joint_weight, output_weight, vectors):
    return (
        lax.all_gather(joint_weight, ("batch", "seq"), axis=0, tiled=True),
        lax.all_gather(output_weight, ("batch", "seq"), axis=0, tiled=True),
        lax.all_gather(vectors, ("batch", "seq"), axis=1, tiled=True),
    )


def gather_feed(expand_weight, reduce_weight, expand_bias):
    return (
        lax.all_gather(expand_weight, ("batch", "seq"), axis=0, tiled=True),
        lax.all_gather(reduce_weight, ("batch", "seq"), axis=0, tiled=True),
        lax.all_gather(expand_bias, ("batch", "seq"), axis=0, tiled=True),
    )


def on_device(
    inputs,
    cotangent,
    lengths,
    joint_weight,
    output_weight,
    vectors,
    expand_weight,
    expand_bias,
    reduce_weight,
):
    seq_count, row_count, model_width = inputs.shape
    head_count = HEADS
    head_size = HEAD_DIM
    tokens = seq_count * row_count
    head_shape = (seq_count, row_count, head_count, head_size)
    own_places = lax.axis_index("seq") * row_count + jnp.arange(row_count, dtype=jnp.int32)
    row_valid = own_places[None, :] < lengths[:, None]
    row_mask = row_valid.reshape(tokens, 1).astype(jnp.float32)
    full_joint, full_output, full_vectors = gather_attention(joint_weight, output_weight, vectors)
    vector_rows = full_vectors.astype(jnp.float32)
    flat_inputs = inputs.reshape(tokens, model_width)
    input_low = flat_inputs.astype(jnp.bfloat16)
    projected = jnp.dot(input_low, full_joint, preferred_element_type=jnp.float32)
    query_low = (projected[:, :model_width] + vector_rows[2]).astype(jnp.bfloat16)
    key_low = projected[:, model_width : 2 * model_width].astype(jnp.bfloat16)
    value_low = (projected[:, 2 * model_width :] + vector_rows[3]).astype(jnp.bfloat16)
    query_heads = query_low.reshape(head_shape)
    key_rows = key_low.reshape(seq_count, row_count, model_width)
    value_rows = value_low.reshape(seq_count, row_count, model_width)
    start_state = (
        jnp.full((seq_count, head_count, row_count), NEG_FILL, jnp.float32),
        jnp.zeros((seq_count, head_count, row_count), jnp.float32),
        jnp.zeros(head_shape, jnp.float32),
    )
    key_piece = lax.all_gather(key_rows, "seq", axis=1, tiled=True)
    value_piece = lax.all_gather(value_rows, "seq", axis=1, tiled=True)

    def forward_score_block(current, offset, block_size):
        running_max, running_sum, summed = current
        key_heads = cut_heads(key_piece, offset, block_size, head_count)
        value_heads = cut_heads(value_piece, offset, block_size, head_count)
        key_places = offset + jnp.arange(block_size, dtype=jnp.int32)
        scores = head_scores(query_heads, key_heads, key_places, lengths)
        new_max = jnp.maximum(running_max, jnp.max(scores, axis=-1))
        factor = jnp.exp(running_max - new_max)
        exp_scores = jnp.exp(scores - new_max[..., None])
        running_sum = running_sum * factor + jnp.sum(exp_scores, axis=-1)
        update = jnp.einsum(
            "shqk,skhd->sqhd",
            exp_scores.astype(jnp.bfloat16),
            value_heads,
            preferred_element_type=jnp.float32,
        )
        summed = summed * jnp.transpose(factor, (0, 2, 1))[..., None] + update
        return (new_max, running_sum, summed)

    running_max, running_sum, summed = over_blocks(
        key_piece.shape[1], forward_score_block, start_state
    )
    attended = summed / jnp.transpose(running_sum, (0, 2, 1))[..., None]
    log_total = jnp.transpose(running_max + jnp.log(running_sum), (0, 2, 1))
    context_low = attended.reshape(tokens, model_width).astype(jnp.bfloat16)
    branch = jnp.dot(context_low, full_output, preferred_element_type=jnp.float32) + vector_rows[4]
    first, first_normed, first_inverse = layer_norm(
        flat_inputs + branch, vector_rows[0], vector_rows[1]
    )
    first_low = first.astype(jnp.bfloat16)
    full_expand, full_reduce, full_bias = gather_feed(expand_weight, reduce_weight, expand_bias)
    before_gelu = jnp.dot(
        first_low, full_expand, preferred_element_type=jnp.float32
    ) + full_bias.astype(jnp.float32)
    hidden_low = gelu_value(before_gelu).astype(jnp.bfloat16)
    feed = jnp.dot(hidden_low, full_reduce, preferred_element_type=jnp.float32) + vector_rows[7]
    result, second_normed, second_inverse = layer_norm(first + feed, vector_rows[5], vector_rows[6])
    full_expand, full_reduce, full_bias = gather_feed(expand_weight, reduce_weight, expand_bias)
    full_joint, full_output, full_vectors = gather_attention(joint_weight, output_weight, vectors)
    grad_res = cotangent.reshape(tokens, model_width) * row_mask
    grad_second, grad_gain_two, grad_shift_two = norm_back(
        grad_res, second_normed, second_inverse, vector_rows[5]
    )
    grad_feed_low = grad_second.astype(jnp.bfloat16)
    grad_reduce_local = jnp.dot(hidden_low.T, grad_feed_low, preferred_element_type=jnp.float32)
    grad_hidden = jnp.dot(
        grad_feed_low, full_reduce.T, preferred_element_type=jnp.float32
    ) * gelu_slope(before_gelu)
    grad_hidden_low = grad_hidden.astype(jnp.bfloat16)
    grad_expand_local = jnp.dot(first_low.T, grad_hidden_low, preferred_element_type=jnp.float32)
    grad_bias_local = jnp.sum(grad_hidden_low.astype(jnp.float32), axis=0)
    grad_first = grad_second + jnp.dot(
        grad_hidden_low, full_expand.T, preferred_element_type=jnp.float32
    )
    grad_resid, grad_gain_one, grad_shift_one = norm_back(
        grad_first, first_normed, first_inverse, vector_rows[0]
    )
    grad_branch_low = grad_resid.astype(jnp.bfloat16)
    grad_output_local = jnp.dot(context_low.T, grad_branch_low, preferred_element_type=jnp.float32)
    grad_context_low = jnp.dot(
        grad_branch_low, full_output.T, preferred_element_type=jnp.float32
    ).astype(jnp.bfloat16)
    grad_context_heads = grad_context_low.reshape(head_shape)
    row_delta = jnp.sum(grad_context_heads.astype(jnp.float32) * attended, axis=-1)
    log_heads = jnp.transpose(log_total, (0, 2, 1))
    delta_heads = jnp.transpose(row_delta, (0, 2, 1))
    query_key_piece = lax.all_gather(key_rows, "seq", axis=1, tiled=True)
    query_value_piece = lax.all_gather(value_rows, "seq", axis=1, tiled=True)

    def query_score_block(current, offset, block_size):
        key_heads = cut_heads(query_key_piece, offset, block_size, head_count)
        value_heads = cut_heads(query_value_piece, offset, block_size, head_count)
        key_places = offset + jnp.arange(block_size, dtype=jnp.int32)
        scores = head_scores(query_heads, key_heads, key_places, lengths)
        softmax_rows = jnp.exp(scores - log_heads[..., None])
        grad_probs = jnp.einsum(
            "sqhd,skhd->shqk", grad_context_heads, value_heads, preferred_element_type=jnp.float32
        )
        grad_scores = (softmax_rows * (grad_probs - delta_heads[..., None])).astype(jnp.bfloat16)
        return (
            current
            + jnp.einsum(
                "shqk,skhd->sqhd", grad_scores, key_heads, preferred_element_type=jnp.float32
            )
            * SCORE_SCALE
        )

    grad_query = over_blocks(
        query_key_piece.shape[1], query_score_block, jnp.zeros(head_shape, jnp.float32)
    )
    own_keys = key_low.reshape(head_shape)
    own_values = value_low.reshape(head_shape)
    query_rows = query_low.reshape(seq_count, row_count, model_width)
    grad_context_rows = grad_context_low.reshape(seq_count, row_count, model_width)
    zero_heads = jnp.zeros(head_shape, jnp.float32)
    query_piece = lax.all_gather(query_rows.astype(jnp.float32), "seq", axis=1, tiled=True).astype(
        jnp.bfloat16
    )
    grad_piece = lax.all_gather(
        grad_context_rows.astype(jnp.float32), "seq", axis=1, tiled=True
    ).astype(jnp.bfloat16)
    log_piece = lax.all_gather(log_total, "seq", axis=1, tiled=True)
    delta_piece = lax.all_gather(row_delta, "seq", axis=1, tiled=True)

    def key_score_block(current, offset, block_size):
        grad_key, grad_value = current
        query_block = cut_heads(query_piece, offset, block_size, head_count)
        grad_block = cut_heads(grad_piece, offset, block_size, head_count)
        log_block = jnp.transpose(
            lax.dynamic_slice_in_dim(log_piece, offset, block_size, 1), (0, 2, 1)
        )
        delta_block = jnp.transpose(
            lax.dynamic_slice_in_dim(delta_piece, offset, block_size, 1), (0, 2, 1)
        )
        scores = head_scores(query_block, own_keys, own_places, lengths)
        softmax_rows = jnp.exp(scores - log_block[..., None])
        grad_value = grad_value + jnp.einsum(
            "shqk,sqhd->skhd",
            softmax_rows.astype(jnp.bfloat16),
            grad_block,
            preferred_element_type=jnp.float32,
        )
        grad_probs = jnp.einsum(
            "sqhd,skhd->shqk", grad_block, own_values, preferred_element_type=jnp.float32
        )
        grad_scores = (softmax_rows * (grad_probs - delta_block[..., None])).astype(jnp.bfloat16)
        grad_key = (
            grad_key
            + jnp.einsum(
                "shqk,sqhd->skhd", grad_scores, query_block, preferred_element_type=jnp.float32
            )
            * SCORE_SCALE
        )
        return (grad_key, grad_value)

    grad_key, grad_value = over_blocks(
        query_piece.shape[1], key_score_block, (zero_heads, zero_heads)
    )
    grad_query_low = grad_query.reshape(tokens, model_width).astype(jnp.bfloat16)
    grad_key_low = grad_key.reshape(tokens, model_width).astype(jnp.bfloat16)
    grad_value_low = grad_value.reshape(tokens, model_width).astype(jnp.bfloat16)
    grad_projected = jnp.concatenate([grad_query_low, grad_key_low, grad_value_low], axis=1)
    grad_joint_local = jnp.dot(input_low.T, grad_projected, preferred_element_type=jnp.float32)
    grad_inputs = grad_resid + jnp.dot(
        grad_projected, full_joint.T, preferred_element_type=jnp.float32
    )
    grad_vector_local = jnp.stack(
        [
            grad_gain_one,
            grad_shift_one,
            jnp.sum(grad_query_low.astype(jnp.float32), axis=0),
            jnp.sum(grad_value_low.astype(jnp.float32), axis=0),
            jnp.sum(grad_branch_low.astype(jnp.float32), axis=0),
            grad_gain_two,
            grad_shift_two,
            jnp.sum(grad_feed_low.astype(jnp.float32), axis=0),
        ],
        axis=0,
    )
    every_grad = (
        lax.psum_scatter(grad_joint_local, ("batch", "seq"), scatter_dimension=0, tiled=True),
        lax.psum_scatter(grad_output_local, ("batch", "seq"), scatter_dimension=0, tiled=True),
        lax.psum_scatter(grad_vector_local, ("batch", "seq"), scatter_dimension=1, tiled=True),
        lax.psum_scatter(grad_expand_local, ("batch", "seq"), scatter_dimension=0, tiled=True),
        lax.psum_scatter(grad_reduce_local, ("batch", "seq"), scatter_dimension=0, tiled=True),
        lax.psum_scatter(grad_bias_local, ("batch", "seq"), scatter_dimension=0, tiled=True),
    )
    summed_grads = (
        every_grad[0],
        every_grad[1],
        every_grad[2],
        every_grad[3],
        every_grad[5],
        every_grad[4],
    )
    return (
        result.reshape(seq_count, row_count, model_width),
        grad_inputs.reshape(seq_count, row_count, model_width),
        summed_grads[0],
        summed_grads[1],
        summed_grads[2],
        summed_grads[3],
        summed_grads[4],
        summed_grads[5],
    )


def solution(mesh):
    return jax.shard_map(
        on_device,
        mesh=mesh,
        in_specs=(
            P("batch", "seq", None),
            P("batch", "seq", None),
            P("batch"),
            P(("batch", "seq"), None),
            P(("batch", "seq"), None),
            P(None, ("batch", "seq")),
            P(("batch", "seq"), None),
            P(("batch", "seq")),
            P(("batch", "seq"), None),
        ),
        out_specs=(
            P("batch", "seq", None),
            P("batch", "seq", None),
            P(("batch", "seq"), None),
            P(("batch", "seq"), None),
            P(None, ("batch", "seq")),
            P(("batch", "seq"), None),
            P(("batch", "seq")),
            P(("batch", "seq"), None),
        ),
        check_vma=False,
    )
```

profile of v0, /device:TPU:0, one launch (start us, length us, event | category | flops | bytes accessed | tf_op | source)
XLA Modules:
  0.0 933.9 jit_solution(14947603904513098469)
XLA Ops:
  9.1 64.5 %all-gather.10.cloned.1.call-done = bf16[768,2304]{1,0:T(8,128)(2,1)} async-done(((bf16[24,2304]{1,0:T(8,128)(2,1)}), bf16[768,2304]{1,0:T(8,128)(2,1)}) %all-gather.10.cloned.1.call-update) | async-done | bytes 3538960 | tf_op jit(solution)/shard_map/all_gather | solution.py:68
  73.7 3.1 fusion.78
  77.9 42.5 %all-gather = bf16[32,24,8]{1,2,0:T(8,128)(2,1)} all-gather(bf16[1,24,8]{1,2,0:T(8,128)(2,1)S(1)} %bitcast.230), channel_id=1, replica_groups=mesh['batch'=4,'seq'=8] {'batch','seq'}, dimensions={0}, use_global_device_ids=true | all-gather | bytes 12672 | tf_op jit(solution)/shard_map/all_gather | solution.py:70
  131.3 37.1 %all-reduce = bf16[3072]{0:T(1024)(128)(2,1)S(1)} all-reduce(bf16[3072]{0:T(1024)(128)(2,1)S(1)} %dynamic-update-slice), channel_id=1, replica_groups=mesh['batch'=4,'seq'=8] {'batch','seq'}, use_global_device_ids=true, to_apply=%add | all-reduce | flops 3072 | bytes 12288
  175.0 38.4 %while.48 = (s32[]{:T(128)}, f32[2,12,128]{2,1,0:T(8,128)S(1)}, f32[2,12,128]{2,1,0:T(8,128)}, f32[2,128,12,64]{1,3,2,0:T(8,128)}, s32[2]{0:T(128)}, /*index=5*/...) while((s32[]{:T(128)}, f32[2,12,128]{2,1,0:T(8,128)S(1)}, ...), condition=%wide.region_3.4_spmd.clone, body=%wide.region_0.3_spmd.clone.sunk | while | flops 210586368 | bytes 25862536 | solution.py:49
  176.4 2.4 constant_dynamic-slice_fusion.12
  185.9 2.4 constant_dynamic-slice_fusion.12
  195.5 2.4 constant_dynamic-slice_fusion.12
  205.1 2.4 constant_dynamic-slice_fusion.12
  214.2 2.9 fusion.73
  219.4 60.8 %all-gather.18.cloned.1.call-done = bf16[768,3072]{1,0:T(8,128)(2,1)} async-done(((bf16[24,3072]{1,0:T(8,128)(2,1)}), bf16[768,3072]{1,0:T(8,128)(2,1)}) %all-gather.18.cloned.1.call-update) | async-done | bytes 4718608 | tf_op jit(solution)/shard_map/all_gather | solution.py:76
  280.2 6.1 multiply_convert_fusion.2
  286.3 59.1 %all-gather.20.cloned.1.call-done = bf16[3072,768]{1,0:T(8,128)(2,1)} async-done(((bf16[96,768]{1,0:T(8,128)(2,1)}), bf16[3072,768]{1,0:T(8,128)(2,1)}) %all-gather.20.cloned.1.call-update) | async-done | bytes 4718608 | tf_op jit(solution)/shard_map/all_gather | solution.py:77
  345.5 4.4 fusion.75
  353.0 3.0 convert_reduce_fusion
  362.9 6.7 fusion.70
  375.6 5.1 fusion.66
  380.8 34.9 %while.49 = (s32[]{:T(128)}, f32[2,128,12,64]{1,3,2,0:T(8,128)}, bf16[2,1024,768]{1,2,0:T(8,128)(2,1)}, s32[2]{0:T(128)}, bf16[2,128,12,64]{1,3,2,0:T(8,128)(2,1...) while((s32[]{:T(128)}, f32[2,128,12,64]{1,3,2,0:T(8,128)}, ...), condition=%wide.region_14.15_spmd.clone, body=%wide.region_13.14_spmd.clone.sunk | while | flops 307299072 | bytes 17329384 | solution.py:49
  380.8 2.4 constant_dynamic-slice_fusion.13
  385.5 3.8 fusion.148
  389.3 2.4 constant_dynamic-slice_fusion.13
  393.9 4.1 fusion.148
  398.0 2.4 constant_dynamic-slice_fusion.13
  402.7 4.1 fusion.148
  406.7 2.4 constant_dynamic-slice_fusion.13
  411.4 4.2 fusion.148
  418.0 10.1 %all_gather.53 = f32[2,1024,12]{1,0,2:T(2,128)} all-gather(f32[2,128,12]{1,0,2:T(2,128)S(1)} %copy-done.29), channel_id=1, replica_groups=mesh['batch'=4,'seq'=8] {'seq'}, dimensions={1}, use_global_device_ids=true | all-gather | bytes 110592 | tf_op jit(solution)/shard_map/all_gather | solution.py:222
  428.1 10.4 %all_gather.51 = f32[2,1024,12]{1,2,0:T(8,128)} all-gather(f32[2,128,12]{1,2,0:T(8,128)} %bitcast.229), channel_id=1, replica_groups=mesh['batch'=4,'seq'=8] {'seq'}, dimensions={1}, use_global_device_ids=true | all-gather | bytes 110592 | tf_op jit(solution)/shard_map/all_gather | solution.py:221
  439.3 57.5 %while.50 = (s32[]{:T(128)}, f32[2,128,12,64]{1,3,2,0:T(8,128)}, f32[2,128,12,64]{1,3,2,0:T(8,128)}, bf16[2,1024,768]{1,2,0:T(8,128)(2,1)}, s32[2]{0:T(128)}, /*...) while((s32[]{:T(128)}, f32[2,128,12,64]{1,3,2,0:T(8,128)}, ...), condition=%wide.region_16.17_spmd.clone, body=%wide.region_15.16_spmd.clone.sunk | while | flops 411500928 | bytes 24602652 | solution.py:49
  439.3 2.5 constant_dynamic-slice_fusion.14
  445.5 4.7 fusion.157
  450.2 3.2 fusion.158
  453.3 2.5 constant_dynamic-slice_fusion.14
  459.5 4.9 fusion.157
  464.4 3.4 fusion.158
  467.8 2.4 constant_dynamic-slice_fusion.14
  474.0 4.9 fusion.157
  478.9 3.4 fusion.158
  482.4 2.4 constant_dynamic-slice_fusion.14
  488.5 4.9 fusion.157
  493.4 3.4 fusion.158
  500.5 3.9 convolution_bitcast_fusion
  504.4 8.1 copy.96
  513.4 40.3 %all-reduce.3 = (f32[8,768]{1,0:T(8,128)S(1)}, f32[3072]{0:T(1024)S(1)}) all-reduce(f32[8,768]{1,0:T(8,128)S(1)} %stack.35, f32[3072]{0:T(1024)S(1)} %copy-done.41), channel_id=4, replica_groups=mesh['batch'=4,'seq'=8] {'batch','seq'}, use_global_device_ids=true, to_apply=%region_27.28.clone | all-reduce | flops 9216 | bytes 73728
  555.0 4.2 convolution_add_fusion.2
  559.2 101.4 %reduce-scatter.10.cloned.1.call-done = f32[24,3072]{1,0:T(8,128)} async-done(((f32[768,3072]{1,0:T(8,128)}), f32[24,3072]{1,0:T(8,128)}) %reduce-scatter.10.cloned.1.call-update) | async-done | bytes 294928 | tf_op jit(solution)/shard_map/reduce_scatter | solution.py:283
  660.6 140.9 %reduce-scatter.12.cloned.1.call-done = f32[96,768]{1,0:T(8,128)} async-done(((f32[3072,768]{1,0:T(8,128)}), f32[96,768]{1,0:T(8,128)}) %reduce-scatter.12.cloned.1.call-update) | async-done | bytes 294928 | tf_op jit(solution)/shard_map/reduce_scatter | solution.py:284
  801.5 125.5 %reduce-scatter.14.cloned.1.call-done = f32[24,2304]{1,0:T(8,128)} async-done(((f32[768,2304]{1,0:T(8,128)}), f32[24,2304]{1,0:T(8,128)}) %reduce-scatter.14.cloned.1.call-update) | async-done | bytes 221200
  (337 shorter events, 100.8 us)
Async XLA Ops:
  7.2 66.5 %all-gather.10.cloned.1.call-start = ((), (), s32[]{:S(2)}) async-start(), calls=%async_computation.4 | async-start | bytes 3649536 | tf_op jit(solution)/shard_map/all_gather | solution.py:68
  7.9 167.1 %all-gather.12.cloned.1.call-start = ((), (), s32[]{:S(2)}) async-start(), calls=%async_computation.5 | async-start | bytes 3538944 | tf_op jit(solution)/shard_map/all_gather | solution.py:117
  9.1 64.6 %copy-start.9 = (bf16[256,768]{1,0:T(8,128)(2,1)}, bf16[256,768]{1,0:T(8,128)(2,1)S(1)}, u32[]{:S(2)}) copy-start(bf16[256,768]{1,0:T(8,128)(2,1)S(1)} %bitcast_convert_fusion) | copy-start | bytes 1179652
  9.1 68.7 %copy-start.47 = (bf16[8,24]{1,0:T(8,128)(2,1)S(1)}, bf16[8,24]{1,0:T(8,128)(2,1)}, u32[]{:S(2)}) copy-start(bf16[8,24]{1,0:T(8,128)(2,1)} %param.20) | copy-start | bytes 1156
  76.8 93.5 %copy-start.4 = (f32[2,128,768]{2,1,0:T(8,128)S(1)}, f32[2,128,768]{2,1,0:T(8,128)}, u32[]{:S(2)}) copy-start(f32[2,128,768]{2,1,0:T(8,128)} %param.16) | copy-start | bytes 2359300
  76.8 49.9 %copy-start.14 = (bf16[256,768]{1,0:T(8,128)(2,1)}, bf16[256,768]{1,0:T(8,128)(2,1)S(1)}, u32[]{:S(2)}) copy-start(bf16[256,768]{1,0:T(8,128)(2,1)S(1)} %slice.73) | copy-start | bytes 1179652
  77.8 97.2 %all-gather.14.cloned.1.call-start = ((), (), s32[]{:S(2)}) async-start(), calls=%async_computation.6 | async-start | bytes 3538944 | tf_op jit(solution)/shard_map/all_gather | solution.py:118
  127.7 47.3 %copy-start.11 = (bf16[256,768]{1,0:T(8,128)(2,1)}, bf16[256,768]{1,0:T(8,128)(2,1)S(1)}, u32[]{:S(2)}) copy-start(bf16[256,768]{1,0:T(8,128)(2,1)S(1)} %get-tuple-element.821) | copy-start | bytes 1179652
  127.7 46.1 %copy-start.13 = (bf16[256,768]{1,0:T(8,128)(2,1)S(1)}, bf16[256,768]{1,0:T(8,128)(2,1)}, u32[]{:S(2)}) copy-start(bf16[256,768]{1,0:T(8,128)(2,1)} %get-tuple-element.822) | copy-start | bytes 1179652
  128.6 88.4 %all-gather.16.cloned.1.call-start = ((), (), s32[]{:S(2)}) async-start(), calls=%async_computation.7 | async-start | bytes 1216512 | tf_op jit(solution)/shard_map/all_gather | solution.py:69
  129.2 151.0 %all-gather.18.cloned.1.call-start = ((), (), s32[]{:S(2)}) async-start(), calls=%async_computation.8 | async-start | bytes 4866048 | tf_op jit(solution)/shard_map/all_gather | solution.py:76
  129.8 215.7 %all-gather.20.cloned.1.call-start = ((), (), s32[]{:S(2)}) async-start(), calls=%async_computation.9 | async-start | bytes 4866048 | tf_op jit(solution)/shard_map/all_gather | solution.py:77
  130.4 308.9 %all-gather.22.cloned.1.call-start = ((), (), s32[]{:S(2)}) async-start(), calls=%async_computation.10 | async-start | bytes 3538944 | tf_op jit(solution)/shard_map/all_gather | solution.py:215
  174.7 264.6 %all-gather.24.cloned.1.call-start = ((), (), s32[]{:S(2)}) async-start(), calls=%async_computation.11 | async-start | bytes 3538944 | tf_op jit(solution)/shard_map/all_gather | solution.py:218
  213.4 66.8 %copy-start.27 = (f32[768]{0:T(1024)S(1)}, f32[768]{0:T(1024)}, u32[]{:S(2)}) copy-start(f32[768]{0:T(1024)} %get-tuple-element.737) | copy-start | bytes 9220
  213.4 66.8 %copy-start.30 = (f32[768]{0:T(1024)S(1)}, f32[768]{0:T(1024)}, u32[]{:S(2)}) copy-start(f32[768]{0:T(1024)} %get-tuple-element.736) | copy-start | bytes 9220
  213.4 66.8 %copy-start.40 = (f32[3072]{0:T(1024)S(1)}, f32[3072]{0:T(1024)}, u32[]{:S(2)}) copy-start(f32[3072]{0:T(1024)} %convert_element_type.147) | copy-start | bytes 36868
  219.2 139.1 %copy-start.33 = (f32[256]{0:T(256)}, f32[256]{0:T(256)S(1)}, u32[]{:S(2)}) copy-start(f32[256]{0:T(256)S(1)} %broadcast_multiply_fusion.4) | copy-start | bytes 3076
  219.4 138.9 %copy-start.39 = (f32[256]{0:T(256)}, f32[256]{0:T(256)S(1)}, u32[]{:S(2)}) copy-start(f32[256]{0:T(256)S(1)} %add_rsqrt_fusion.1) | copy-start | bytes 3076
  280.2 65.2 %copy-start.44 = (f32[768]{0:T(1024)S(1)}, f32[768]{0:T(1024)}, u32[]{:S(2)}) copy-start(f32[768]{0:T(1024)} %get-tuple-element.735) | copy-start | bytes 9220
  345.5 7.5 slice-start.2
  345.5 4.8 copy-start.5
  345.5 4.8 copy-start.31
  345.5 4.8 copy-start.42
  345.5 5.7 copy-start.34
  345.5 5.7 copy-start.43
  345.5 7.5 slice-start.3
  350.0 3.1 copy-start.48
  351.1 4.9 slice-start
  353.0 3.0 slice-start.1
  356.0 3.1 copy-start.8
  359.1 3.4 copy-start.6
  360.6 198.6 %reduce-scatter.8.cloned.1.call-start = ((), (), s32[]{:S(2)}) async-start(), calls=%async_computation.12 | async-start | bytes 2433024 | tf_op jit(solution)/shard_map/reduce_scatter | solution.py:281
  362.6 298.0 %reduce-scatter.10.cloned.1.call-start = ((), (), s32[]{:S(2)}) async-start(), calls=%async_computation.13 | async-start | bytes 9732096 | tf_op jit(solution)/shard_map/reduce_scatter | solution.py:283
  369.6 432.0 %reduce-scatter.12.cloned.1.call-start = ((), (), s32[]{:S(2)}) async-start(), calls=%async_computation.14 | async-start | bytes 9732096 | tf_op jit(solution)/shard_map/reduce_scatter | solution.py:284
  370.7 3.2 copy-start.17
  371.0 4.0 copy-start.22
  373.1 2.5 copy-start.18
  374.4 6.3 copy-start.28
  380.7 546.3 %reduce-scatter.14.cloned.1.call-start = ((), (), s32[]{:S(2)}) async-start(), calls=%async_computation.15 | async-start | bytes 7299072
  380.8 37.2 %copy-start.29 = (f32[2,128,12]{1,0,2:T(2,128)S(1)}, f32[2,128,12]{1,0,2:T(2,128)}, u32[]{:S(2)}) copy-start(f32[2,128,12]{1,0,2:T(2,128)} %copy-done.28) | copy-start | bytes 36868
  439.3 3.3 copy-start.3
  453.3 3.3 copy-start.3
  467.8 3.3 copy-start.3
  482.4 3.3 copy-start.3
  496.8 3.5 copy-start.16
  496.8 3.6 copy-start.10
  512.5 42.5 %copy-start.7 = (f32[256,768]{1,0:T(8,128)S(1)}, f32[256,768]{1,0:T(8,128)}, u32[]{:S(2)}) copy-start(f32[256,768]{1,0:T(8,128)} %copy-done.6) | copy-start | bytes 2359300
  (47 other events, 73.4 us)
Sparse Core Ops, SparseCore 0:
  10.9 62.7 all-gather.9
  77.9 31.7 all-gather.11
  128.7 29.0 all-gather.13
  160.6 54.1 all-gather.15
  217.6 62.5 all-gather.17
  283.0 62.4 all-gather.19
  347.3 31.6 all-gather.21
  380.9 32.8 all-gather.23
  419.6 99.0 reduce-scatter.7
  526.0 134.5 reduce-scatter.9
  667.1 134.4 reduce-scatter.11
  808.6 118.3 reduce-scatter.13
where the time goes:
time: 937 us; the launch traced here: 934 us
  waiting for transfers between devices  555 us (59%)
  blocking collectives  140 us (15%)
  matrix products  108 us (12%)
  local copies, waits for them, and re-layouts  76 us (8%)
  other arithmetic  39 us (4%)
  between operations  14.8 us (2%)
    reduce_scatter x1, waiting for transfers between devices, on_device(): lax.psum_scatter(grad_reduce_local, ('batch', 'seq'), scatter_dimension=0...  141 us
    unnamed x13, waiting for transfers between devices  128 us
    reduce_scatter x1, waiting for transfers between devices, on_device(): lax.psum_scatter(grad_expand_local, ('batch', 'seq'), scatter_dimension=0...  101 us
    unnamed x2, blocking collectives  77.4 us
    all_gather x1, waiting for transfers between devices, gather_attention(): lax.all_gather(joint_weight, ('batch', 'seq'), axis=0, tiled=True)  64.5 us
    all_gather x1, waiting for transfers between devices, gather_feed(): lax.all_gather(expand_weight, ('batch', 'seq'), axis=0, tiled=True)  60.8 us
    all_gather x1, waiting for transfers between devices, gather_feed(): lax.all_gather(reduce_weight, ('batch', 'seq'), axis=0, tiled=True)  59.1 us
    all_gather x1, blocking collectives, gather_attention(): lax.all_gather(vectors, ('batch', 'seq'), axis=1, tiled=True)  42.5 us
  transfers between devices with their start and end apart: 12, of which 6 were waited for; matrix products, arithmetic and copies ran while one was open for 22% of the time, Pallas kernels for 0%

commit v1 on v0

--- a/solution.py
+++ b/solution.py
@@ -3,6 +3,7 @@
 import jax.numpy as jnp
 from jax import lax
 from jax.sharding import PartitionSpec as P
+from jax.lax import axis_index, axis_size, ppermute
 
 HEADS = 12
 HEAD_DIM = 64
@@ -72,8 +73,25 @@
 
 
 def gather_feed(expand_weight, reduce_weight, expand_bias):
+
+    def choose_windows(local_x, mesh_ax):
+        raw_out = axis_size(mesh_ax)
+        tall = axis_index(mesh_ax)
+        x_now, b_next = (raw_out, tall)
+        y1, taken_in = (local_x, 1)
+        while taken_in < x_now:
+            b_now = range(x_now)
+            v1 = map(lambda u: (u, u ^ taken_in), b_now)
+            y2 = list(v1)
+            y = ppermute(y1, mesh_ax, y2)
+            carry = jnp.concatenate([y1, y], axis=0)
+            a_now = jnp.concatenate([y, y1], axis=0)
+            y1 = jnp.where(b_next & taken_in == 0, carry, a_now)
+            taken_in = 2 * taken_in
+        return y1
+
     return (
-        lax.all_gather(expand_weight, ("batch", "seq"), axis=0, tiled=True),
+        choose_windows(expand_weight, ("batch", "seq")),
         lax.all_gather(reduce_weight, ("batch", "seq"), axis=0, tiled=True),
         lax.all_gather(expand_bias, ("batch", "seq"), axis=0, tiled=True),
     )

time: 937 us -> 956 us (1.020)
    ppermute x0 -> x5, waiting for transfers between devices: none -> 98.1 us  [choose_windows(): y = ppermute(y1, mesh_ax, y2)]
    all_gather x1 -> x0, waiting for transfers between devices: 60.8 us -> none  [gather_feed(): lax.all_gather(expand_weight, ('batch', 'seq'), axis=0, tiled=True)]
    all_gather x1, waiting for transfers between devices: 59.1 us -> 36.1 us  [gather_feed(): lax.all_gather(reduce_weight, ('batch', 'seq'), axis=0, tiled=True)]
    unnamed x13 -> x12, waiting for transfers between devices: 128 us -> 127 us
  transfers between devices with their start and end apart: 12 -> 16, of which waited for: 6 -> 9; matrix products, arithmetic and copies ran while one was open for 22% -> 22% of each run, Pallas kernels for 0% -> 0%
where the time goes in v1:
time: 956 us; the launch traced here: 953 us
  waiting for transfers between devices  564 us (59%)
  blocking collectives  147 us (15%)
  matrix products  112 us (12%)
  local copies, waits for them, and re-layouts  69.9 us (7%)
  other arithmetic  42.5 us (4%)
  between operations  14.6 us (2%)
    reduce_scatter x1, waiting for transfers between devices, on_device(): lax.psum_scatter(grad_reduce_local, ('batch', 'seq'), scatter_dimension=0...  141 us
    unnamed x12, waiting for transfers between devices  127 us
    ppermute x5, waiting for transfers between devices, choose_windows(): y = ppermute(y1, mesh_ax, y2)  98.1 us
    reduce_scatter x1, waiting for transfers between devices, on_device(): lax.psum_scatter(grad_expand_local, ('batch', 'seq'), scatter_dimension=0...  97.3 us
    unnamed x2, blocking collectives  86.6 us
    all_gather x1, waiting for transfers between devices, gather_attention(): lax.all_gather(joint_weight, ('batch', 'seq'), axis=0, tiled=True)  64.5 us
    all_gather x1, blocking collectives, gather_attention(): lax.all_gather(vectors, ('batch', 'seq'), axis=1, tiled=True)  39.9 us
    all_gather x1, waiting for transfers between devices, gather_feed(): lax.all_gather(reduce_weight, ('batch', 'seq'), axis=0, tiled=True)  36.1 us
  transfers between devices with their start and end apart: 16, of which 9 were waited for; matrix products, arithmetic and copies ran while one was open for 22% of the time, Pallas kernels for 0%

profile of v1, /device:TPU:0, one launch (start us, length us, event | category | flops | bytes accessed | tf_op | source)
XLA Modules:
  0.0 953.4 jit_solution(12444746135876896372)
XLA Ops:
  9.1 64.5 %all-gather.9.cloned.1.call-done = bf16[768,2304]{1,0:T(8,128)(2,1)} async-done(((bf16[24,2304]{1,0:T(8,128)(2,1)}), bf16[768,2304]{1,0:T(8,128)(2,1)}) %all-gather.9.cloned.1.call-update) | async-done | bytes 3538960 | tf_op jit(solution)/shard_map/all_gather | solution.py:69
  73.7 3.1 fusion.80
  77.9 39.9 %all-gather = bf16[32,24,8]{1,2,0:T(8,128)(2,1)S(1)} all-gather(bf16[1,24,8]{1,2,0:T(8,128)(2,1)S(1)} %bitcast.228), channel_id=1, replica_groups=mesh['batch'=4,'seq'=8] {'batch','seq'}, dimensions={0}, use_global_device_ids=true | all-gather | bytes 12672 | tf_op jit(solution)/shard_map/all_gather | solution.py:71
  122.7 13.4 %collective-permute-done.1 = bf16[48,3072]{1,0:T(8,128)(2,1)S(1)} collective-permute-done((bf16[48,3072]{1,0:T(8,128)(2,1)S(1)}, bf16[48,3072]{1,0:T(8,128)(2,1)S(1)}, u32[]{:S(2)}, u32[]{:S(2)}) %collective-permute-start.1) | collective-permute-done | bytes 294944 | tf_op jit(solution)/shard_map/ppermute | solution.py:86
  137.1 22.6 %collective-permute-done.2 = bf16[96,3072]{1,0:T(8,128)(2,1)} collective-permute-done((bf16[96,3072]{1,0:T(8,128)(2,1)S(1)}, bf16[96,3072]{1,0:T(8,128)(2,1)}, u32[]{:S(2)}, u32[]{:S(2)}) %collective-permute-start.2) | collective-permute-done | bytes 589856 | tf_op jit(solution)/shard_map/ppermute | solution.py:86
  162.0 46.4 %all-reduce = bf16[3072]{0:T(1024)(128)(2,1)S(1)} all-reduce(bf16[3072]{0:T(1024)(128)(2,1)S(1)} %dynamic-update-slice), channel_id=1, replica_groups=mesh['batch'=4,'seq'=8] {'batch','seq'}, use_global_device_ids=true, to_apply=%add | all-reduce | flops 3072 | bytes 12288
  211.6 3.1 maximum_select_fusion.1
  217.5 38.2 %while.48 = (s32[]{:T(128)}, f32[2,12,128]{2,1,0:T(8,128)S(1)}, f32[2,12,128]{2,1,0:T(8,128)}, f32[2,128,12,64]{1,3,2,0:T(8,128)}, s32[2]{0:T(128)}, /*index=5*/...) while((s32[]{:T(128)}, f32[2,12,128]{2,1,0:T(8,128)S(1)}, ...), condition=%wide.region_3.4_spmd.clone, body=%wide.region_0.3_spmd.clone.sunk | while | flops 210586368 | bytes 25862536 | solution.py:50
  256.4 2.9 fusion.75
  261.7 61.0 %collective-permute-done.4 = bf16[384,3072]{1,0:T(8,128)(2,1)} collective-permute-done((bf16[384,3072]{1,0:T(8,128)(2,1)}, bf16[384,3072]{1,0:T(8,128)(2,1)}, u32[]{:S(2)}, u32[]{:S(2)}) %collective-permute-start.4) | collective-permute-done | bytes 2359328 | tf_op jit(solution)/shard_map/ppermute | solution.py:86
  322.7 6.6 multiply_convert_fusion.2
  329.4 36.1 %all-gather.17.cloned.1.call-done = bf16[3072,768]{1,0:T(8,128)(2,1)} async-done(((bf16[96,768]{1,0:T(8,128)(2,1)}), bf16[3072,768]{1,0:T(8,128)(2,1)}) %all-gather.17.cloned.1.call-update) | async-done | bytes 4718608 | tf_op jit(solution)/shard_map/all_gather | solution.py:95
  365.5 4.4 fusion.77
  373.0 3.0 convert_reduce_fusion
  376.0 6.2 multiply_reduce_fusion.1
  386.8 6.7 fusion.72
  399.7 5.1 fusion.68
  404.9 34.7 %while.49 = (s32[]{:T(128)}, f32[2,128,12,64]{1,3,2,0:T(8,128)}, bf16[2,1024,768]{1,2,0:T(8,128)(2,1)}, s32[2]{0:T(128)}, bf16[2,128,12,64]{1,3,2,0:T(8,128)(2,1...) while((s32[]{:T(128)}, f32[2,128,12,64]{1,3,2,0:T(8,128)}, ...), condition=%wide.region_14.15_spmd.clone, body=%wide.region_13.14_spmd.clone.sunk | while | flops 307299072 | bytes 17329384 | solution.py:50
  404.9 2.4 constant_dynamic-slice_fusion.13
  409.6 3.8 fusion.148
  413.3 2.4 constant_dynamic-slice_fusion.13
  418.0 4.1 fusion.148
  422.1 2.4 constant_dynamic-slice_fusion.13
  426.8 4.1 fusion.148
  430.8 2.4 constant_dynamic-slice_fusion.13
  435.5 4.1 fusion.148
  441.9 10.2 %all_gather.48 = f32[2,1024,12]{1,0,2:T(2,128)} all-gather(f32[2,128,12]{1,0,2:T(2,128)S(1)} %copy-done.30), channel_id=1, replica_groups=mesh['batch'=4,'seq'=8] {'seq'}, dimensions={1}, use_global_device_ids=true | all-gather | bytes 110592 | tf_op jit(solution)/shard_map/all_gather | solution.py:240
  452.1 10.3 %all_gather.46 = f32[2,1024,12]{1,2,0:T(8,128)} all-gather(f32[2,128,12]{1,2,0:T(8,128)} %bitcast.227), channel_id=1, replica_groups=mesh['batch'=4,'seq'=8] {'seq'}, dimensions={1}, use_global_device_ids=true | all-gather | bytes 110592 | tf_op jit(solution)/shard_map/all_gather | solution.py:239
  463.2 57.7 %while.50 = (s32[]{:T(128)}, f32[2,128,12,64]{1,3,2,0:T(8,128)}, f32[2,128,12,64]{1,3,2,0:T(8,128)}, bf16[2,1024,768]{1,2,0:T(8,128)(2,1)}, s32[2]{0:T(128)}, /*...) while((s32[]{:T(128)}, f32[2,128,12,64]{1,3,2,0:T(8,128)}, ...), condition=%wide.region_16.17_spmd.clone, body=%wide.region_15.16_spmd.clone.sunk | while | flops 411500928 | bytes 24602652 | solution.py:50
  463.2 2.5 constant_dynamic-slice_fusion.14
  469.4 4.7 fusion.157
  474.1 3.2 fusion.158
  477.3 2.5 constant_dynamic-slice_fusion.14
  483.5 4.9 fusion.157
  488.4 3.4 fusion.158
  491.8 2.5 constant_dynamic-slice_fusion.14
  498.0 4.9 fusion.157
  503.0 3.4 fusion.158
  506.4 2.5 constant_dynamic-slice_fusion.14
  512.6 4.9 fusion.157
  517.5 3.4 fusion.158
  524.6 3.9 convolution_bitcast_fusion
  528.5 8.1 copy.96
  537.6 40.2 %all-reduce.3 = (f32[8,768]{1,0:T(8,128)S(1)}, f32[3072]{0:T(1024)S(1)}) all-reduce(f32[8,768]{1,0:T(8,128)S(1)} %stack.35, f32[3072]{0:T(1024)S(1)} %copy-done.43), channel_id=4, replica_groups=mesh['batch'=4,'seq'=8] {'batch','seq'}, use_global_device_ids=true, to_apply=%region_27.28.clone | all-reduce | flops 9216 | bytes 73728
  579.0 4.2 convolution_add_fusion.2
  583.2 97.3 %reduce-scatter.10.cloned.1.call-done = f32[24,3072]{1,0:T(8,128)} async-done(((f32[768,3072]{1,0:T(8,128)}), f32[24,3072]{1,0:T(8,128)}) %reduce-scatter.10.cloned.1.call-update) | async-done | bytes 294928 | tf_op jit(solution)/shard_map/reduce_scatter | solution.py:301
  680.5 140.7 %reduce-scatter.12.cloned.1.call-done = f32[96,768]{1,0:T(8,128)} async-done(((f32[3072,768]{1,0:T(8,128)}), f32[96,768]{1,0:T(8,128)}) %reduce-scatter.12.cloned.1.call-update) | async-done | bytes 294928 | tf_op jit(solution)/shard_map/reduce_scatter | solution.py:302
  821.2 125.6 %reduce-scatter.14.cloned.1.call-done = f32[24,2304]{1,0:T(8,128)} async-done(((f32[768,2304]{1,0:T(8,128)}), f32[24,2304]{1,0:T(8,128)}) %reduce-scatter.14.cloned.1.call-update) | async-done | bytes 221200
  (349 shorter events, 104.3 us)
Async XLA Ops:
  7.2 66.5 %all-gather.9.cloned.1.call-start = ((), (), s32[]{:S(2)}) async-start(), calls=%async_computation.4 | async-start | bytes 3649536 | tf_op jit(solution)/shard_map/all_gather | solution.py:69
  7.9 209.5 %all-gather.11.cloned.1.call-start = ((), (), s32[]{:S(2)}) async-start(), calls=%async_computation.5 | async-start | bytes 3538944 | tf_op jit(solution)/shard_map/all_gather | solution.py:135
  9.1 67.7 %copy-start.9 = (bf16[256,768]{1,0:T(8,128)(2,1)}, bf16[256,768]{1,0:T(8,128)(2,1)S(1)}, u32[]{:S(2)}) copy-start(bf16[256,768]{1,0:T(8,128)(2,1)S(1)} %bitcast_convert_fusion) | copy-start | bytes 1179652
  9.1 68.7 %copy-start.49 = (bf16[8,24]{1,0:T(8,128)(2,1)S(1)}, bf16[8,24]{1,0:T(8,128)(2,1)}, u32[]{:S(2)}) copy-start(bf16[8,24]{1,0:T(8,128)(2,1)} %param.20) | copy-start | bytes 1156
  76.8 44.3 %copy-start.28 = (bf16[24,3072]{1,0:T(8,128)(2,1)S(1)}, bf16[24,3072]{1,0:T(8,128)(2,1)}, u32[]{:S(2)}) copy-start(bf16[24,3072]{1,0:T(8,128)(2,1)} %param.21) | copy-start | bytes 442372
  76.9 41.9 %copy-start.13 = (bf16[256,768]{1,0:T(8,128)(2,1)}, bf16[256,768]{1,0:T(8,128)(2,1)S(1)}, u32[]{:S(2)}) copy-start(bf16[256,768]{1,0:T(8,128)(2,1)S(1)} %slice.73) | copy-start | bytes 1179652
  77.8 139.6 %all-gather.13.cloned.1.call-start = ((), (), s32[]{:S(2)}) async-start(), calls=%async_computation.6 | async-start | bytes 3538944 | tf_op jit(solution)/shard_map/all_gather | solution.py:136
  118.8 91.5 %copy-start.32 = (f32[768]{0:T(1024)}, f32[768]{0:T(1024)S(1)}, u32[]{:S(2)}) copy-start(f32[768]{0:T(1024)S(1)} %get-tuple-element.733) | copy-start | bytes 9220
  118.9 92.2 %copy-start.11 = (bf16[256,768]{1,0:T(8,128)(2,1)}, bf16[256,768]{1,0:T(8,128)(2,1)S(1)}, u32[]{:S(2)}) copy-start(bf16[256,768]{1,0:T(8,128)(2,1)S(1)} %get-tuple-element.821) | copy-start | bytes 1179652
  118.9 42.9 %copy-start.50 = (bf16[96]{0:T(256)(128)(2,1)S(1)}, bf16[96]{0:T(256)(128)(2,1)}, u32[]{:S(2)}) copy-start(bf16[96]{0:T(256)(128)(2,1)} %param.22) | copy-start | bytes 580
  118.9 91.4 %copy-start.4 = (f32[2,128,768]{2,1,0:T(8,128)S(1)}, f32[2,128,768]{2,1,0:T(8,128)}, u32[]{:S(2)}) copy-start(f32[2,128,768]{2,1,0:T(8,128)} %param.16) | copy-start | bytes 2359300
  119.9 139.4 %all-gather.15.cloned.1.call-start = ((), (), s32[]{:S(2)}) async-start(), calls=%async_computation.7 | async-start | bytes 1216512 | tf_op jit(solution)/shard_map/all_gather | solution.py:70
  120.5 245.0 %all-gather.17.cloned.1.call-start = ((), (), s32[]{:S(2)}) async-start(), calls=%async_computation.8 | async-start | bytes 4866048 | tf_op jit(solution)/shard_map/all_gather | solution.py:95
  121.0 342.2 %all-gather.19.cloned.1.call-start = ((), (), s32[]{:S(2)}) async-start(), calls=%async_computation.9 | async-start | bytes 3538944 | tf_op jit(solution)/shard_map/all_gather | solution.py:233
  121.1 1.4 collective-permute-start
  122.6 13.5 %collective-permute-start.1 = (bf16[48,3072]{1,0:T(8,128)(2,1)S(1)}, bf16[48,3072]{1,0:T(8,128)(2,1)S(1)}, u32[]{:S(2)}, u32[]{:S(2)}) collective-permute-start(bf16[48,3072]{1,0:T(8,128)(2,1)S(1)} %maximum_select_fusion.6), channel_id=1, source_target_pairs={{0,2},{1,3},{2,0},{3,1},{4,6},{5,7},{6,4},{7,5},{8,10},{9,11},{10,... | collective-permute-start | bytes 884744 | tf_op jit(solution)/shard_map/ppermute | solution.py:86
  136.3 23.4 %collective-permute-start.2 = (bf16[96,3072]{1,0:T(8,128)(2,1)S(1)}, bf16[96,3072]{1,0:T(8,128)(2,1)}, u32[]{:S(2)}, u32[]{:S(2)}) collective-permute-start(bf16[96,3072]{1,0:T(8,128)(2,1)S(1)} %maximum_select_fusion.5), channel_id=1, source_target_pairs={{0,4},{1,5},{2,6},{3,7},{4,0},{5,1},{6,2},{7,3},{8,12},{9,13},{10,... | collective-permute-start | bytes 1769480 | tf_op jit(solution)/shard_map/ppermute | solution.py:86
  161.6 50.0 %collective-permute-start.3 = (bf16[192,3072]{1,0:T(8,128)(2,1)S(1)}, bf16[192,3072]{1,0:T(8,128)(2,1)}, u32[]{:S(2)}, u32[]{:S(2)}) collective-permute-start(bf16[192,3072]{1,0:T(8,128)(2,1)S(1)} %maximum_select_fusion.2), channel_id=1, source_target_pairs={{0,8},{1,9},{2,10},{3,11},{4,12},{5,13},{6,14},{7,15},{8,0},{9,1},... | collective-permute-start | bytes 3538952 | tf_op jit(solution)/shard_map/ppermute | solution.py:86
  214.7 108.0 %collective-permute-start.4 = (bf16[384,3072]{1,0:T(8,128)(2,1)}, bf16[384,3072]{1,0:T(8,128)(2,1)}, u32[]{:S(2)}, u32[]{:S(2)}) collective-permute-start(bf16[384,3072]{1,0:T(8,128)(2,1)} %maximum_select_fusion.1), channel_id=1, source_target_pairs={{0,16},{1,17},{2,18},{3,19},{4,20},{5,21},{6,22},{7,23},{8,24},{9,... | collective-permute-start | bytes 7077896 | tf_op jit(solution)/shard_map/ppermute | solution.py:86
  217.2 246.0 %all-gather.21.cloned.1.call-start = ((), (), s32[]{:S(2)}) async-start(), calls=%async_computation.10 | async-start | bytes 3538944 | tf_op jit(solution)/shard_map/all_gather | solution.py:236
  255.7 67.0 %copy-start.27 = (f32[768]{0:T(1024)S(1)}, f32[768]{0:T(1024)}, u32[]{:S(2)}) copy-start(f32[768]{0:T(1024)} %get-tuple-element.737) | copy-start | bytes 9220
  255.7 67.0 %copy-start.31 = (f32[768]{0:T(1024)S(1)}, f32[768]{0:T(1024)}, u32[]{:S(2)}) copy-start(f32[768]{0:T(1024)} %get-tuple-element.736) | copy-start | bytes 9220
  255.7 67.0 %copy-start.42 = (f32[3072]{0:T(1024)S(1)}, f32[3072]{0:T(1024)}, u32[]{:S(2)}) copy-start(f32[3072]{0:T(1024)} %convert_element_type.147) | copy-start | bytes 36868
  261.4 120.8 %copy-start.35 = (f32[256]{0:T(256)}, f32[256]{0:T(256)S(1)}, u32[]{:S(2)}) copy-start(f32[256]{0:T(256)S(1)} %broadcast_multiply_fusion.4) | copy-start | bytes 3076
  261.6 120.6 %copy-start.41 = (f32[256]{0:T(256)}, f32[256]{0:T(256)S(1)}, u32[]{:S(2)}) copy-start(f32[256]{0:T(256)S(1)} %add_rsqrt_fusion.1) | copy-start | bytes 3076
  322.7 42.7 %copy-start.46 = (f32[768]{0:T(1024)S(1)}, f32[768]{0:T(1024)}, u32[]{:S(2)}) copy-start(f32[768]{0:T(1024)} %get-tuple-element.735) | copy-start | bytes 9220
  365.4 7.5 slice-start
  365.5 4.7 copy-start.5
  365.5 4.8 copy-start.33
  365.5 4.8 copy-start.44
  365.5 5.7 copy-start.36
  365.5 5.7 copy-start.45
  365.5 7.5 slice-start.1
  376.0 6.2 copy-start.19
  376.0 7.1 copy-start.8
  383.1 3.4 copy-start.6
  384.6 198.6 %reduce-scatter.8.cloned.1.call-start = ((), (), s32[]{:S(2)}) async-start(), calls=%async_computation.11 | async-start | bytes 2433024 | tf_op jit(solution)/shard_map/reduce_scatter | solution.py:299
  386.6 293.9 %reduce-scatter.10.cloned.1.call-start = ((), (), s32[]{:S(2)}) async-start(), calls=%async_computation.12 | async-start | bytes 9732096 | tf_op jit(solution)/shard_map/reduce_scatter | solution.py:301
  393.6 427.6 %reduce-scatter.12.cloned.1.call-start = ((), (), s32[]{:S(2)}) async-start(), calls=%async_computation.13 | async-start | bytes 9732096 | tf_op jit(solution)/shard_map/reduce_scatter | solution.py:302
  395.1 4.0 copy-start.22
  398.4 6.3 copy-start.29
  404.8 542.0 %reduce-scatter.14.cloned.1.call-start = ((), (), s32[]{:S(2)}) async-start(), calls=%async_computation.14 | async-start | bytes 7299072
  404.9 37.0 %copy-start.30 = (f32[2,128,12]{1,0,2:T(2,128)S(1)}, f32[2,128,12]{1,0,2:T(2,128)}, u32[]{:S(2)}) copy-start(f32[2,128,12]{1,0,2:T(2,128)} %copy-done.29) | copy-start | bytes 36868
  463.2 3.4 copy-start.3
  506.4 3.4 copy-start.3
  520.9 3.5 copy-start.15
  520.9 3.6 copy-start.10
  536.6 42.4 %copy-start.7 = (f32[256,768]{1,0:T(8,128)S(1)}, f32[256,768]{1,0:T(8,128)}, u32[]{:S(2)}) copy-start(f32[256,768]{1,0:T(8,128)} %copy-done.6) | copy-start | bytes 2359300
  (52 other events, 87.2 us)
Sparse Core Ops, SparseCore 0:
  10.9 62.7 all-gather.8
  77.9 31.7 all-gather.10
  120.0 40.5 all-gather.12
  163.3 51.5 all-gather.14
  217.6 147.7 all-gather.16
  367.2 31.6 all-gather.18
  400.7 32.8 all-gather.20
  439.4 99.0 reduce-scatter.7
  546.0 134.4 reduce-scatter.9
  686.8 134.3 reduce-scatter.11
  828.4 118.3 reduce-scatter.13
